TPU v7x, 512 devices: a whole 4x4x16 slice. The times are simulated.
512 devices in a mesh: head: 8 (over y, core), seq: 64 (over x, z).
Axes of the slice: x: 4, y: 4, z: 16, core: 2. Of those that a mesh axis runs over, the one named last changes fastest.
Arguments:
- queries: bfloat16 [2, 32768, 8, 256], P(None, 'seq', 'head'), may hold values from -5 to 5
- key_rows: bfloat16 [2, 32768, 8, 256], P(None, 'seq', 'head'), may hold values from -5 to 5
- values: bfloat16 [2, 32768, 8, 256], P(None, 'seq', 'head'), may hold values from -6 to 6
- learn_rates: float32 [8, 2, 32768], P('head', None, 'seq'), may hold values from 0.02 to 0.6, as said below
- fast_gate: float32 [8, 256, 512], P('head'), may hold values from -0.375 to 0.375
- fast_down: float32 [8, 512, 256], P('head'), may hold values from -0.25 to 0.25
- fast_up: float32 [8, 256, 512], P('head'), may hold values from -0.375 to 0.375
- output_weight: bfloat16 [2048, 2048], P(None, ('head', 'seq')), may hold values from -0.125 to 0.125
Outputs:
- output: bfloat16 [2, 32768, 2048], P(None, 'seq', 'head')
Inputs may be any that keep to these rules, and one draw needn't show every extreme that they name: `learn_rates`: learning rates are positive.
All inputs are finite; a program needn't handle non-finite values.
Results may differ from a plain program's by a relative error of at most 0.0095.
Values may be sent and summed in bfloat16 or wider, within the bound.
No kernel may reach another device: no remote copies, remote signals or barrier semaphores. Data moves between devices by JAX's collectives and lax.ppermute only.
A program may use at most 64 MiB of HBM per device.

v0:
```python
import math

import jax
import jax.numpy as jnp
from jax import lax
from jax.sharding import Mesh
from jax.sharding import PartitionSpec as P

WINDOW = 256
SEQ = ("seq_0", "seq_1")
HEAD_SEQ = ("head", "seq_0", "seq_1")


MOMENTUM = 0.9


def passed_along(value, axis, steps):
    count = lax.axis_size(axis)
    pairs = [(source, (source + steps) % count) for source in range(count)]
    return lax.ppermute(value, axis, pairs)


def laid_out(blocks, dim):
    dims = list(blocks.shape[1:])
    dims[dim] *= blocks.shape[0]
    return jnp.moveaxis(blocks, 0, dim).reshape(dims)


def stacked_from(x, axes, turns):
    blocks = x
    for k in turns:
        blocks = lax.all_gather(blocks, axes[k])
    done = turns[::-1]
    back = [done.index(k) for k in range(len(axes))]
    blocks = blocks.transpose(*back, *range(len(axes), blocks.ndim))
    return blocks.reshape(-1, *x.shape)


def whole_of(x, axes, turns, dim):
    return laid_out(stacked_from(x, axes, turns), dim)


def silu_slope(pre_act):
    sigmoid_value = jax.nn.sigmoid(pre_act)
    return sigmoid_value * (1.0 + pre_act * (1.0 - sigmoid_value))


def contract_rows(left, right):
    return lax.dot_general(
        left, right, (((0,), (0,)), ((), ())), preferred_element_type=jnp.float32
    )


def span_gradient(key_span, value_span, rate_span, current):
    gate_low, down_low, up_low = current
    pre_gate = jnp.dot(key_span, gate_low, preferred_element_type=jnp.float32)
    pre_up = jnp.dot(key_span, up_low, preferred_element_type=jnp.float32)
    hidden = (jax.nn.silu(pre_gate) * pre_up).astype(jnp.bfloat16)
    target = (-(rate_span[:, None] * value_span.astype(jnp.float32))).astype(jnp.bfloat16)
    grad_down = contract_rows(hidden, target)
    back_grad = lax.dot_general(
        target, down_low, (((1,), (1,)), ((), ())), preferred_element_type=jnp.float32
    )
    grad_pre_gate = (back_grad * pre_up * silu_slope(pre_gate)).astype(jnp.bfloat16)
    grad_pre_up = (back_grad * jax.nn.silu(pre_gate)).astype(jnp.bfloat16)
    return (contract_rows(key_span, grad_pre_gate), grad_down, contract_rows(key_span, grad_pre_up))


def apply_fast(query_span, current):
    gate_low, down_low, up_low = current
    pre_gate = jnp.dot(query_span, gate_low, preferred_element_type=jnp.float32)
    pre_up = jnp.dot(query_span, up_low, preferred_element_type=jnp.float32)
    hidden = (jax.nn.silu(pre_gate) * pre_up).astype(jnp.bfloat16)
    fast = jnp.dot(hidden, down_low, preferred_element_type=jnp.float32)
    return fast * lax.rsqrt(jnp.mean(fast * fast, axis=-1, keepdims=True) + 1e-05)


def square_sum(members):
    return (
        jnp.sum(members[0] * members[0])
        + jnp.sum(members[1] * members[1])
        + jnp.sum(members[2] * members[2])
    )


def advance(momentum, gradient, factor):
    if momentum is None:
        return tuple((factor * member for member in gradient))
    return tuple(
        (MOMENTUM * earlier + factor * member for earlier, member in zip(momentum, gradient))
    )


def window_attend(query_local, key_local, value_local, edge_pair, seq_index):
    spans, span_rows, head_dim = query_local.shape
    edge_keys, edge_values = edge_pair
    is_first = seq_index == 0
    edge_keys = jnp.where(is_first, jnp.roll(edge_keys, 1, axis=0), edge_keys)
    edge_values = jnp.where(is_first, jnp.roll(edge_values, 1, axis=0), edge_values)
    wide_keys = jnp.concatenate([edge_keys, key_local], axis=1)
    wide_values = jnp.concatenate([edge_values, value_local], axis=1)
    grid_shape = (spans, WINDOW, 2 * WINDOW)
    row_ids = lax.broadcasted_iota(jnp.int32, grid_shape, 1)
    col_ids = lax.broadcasted_iota(jnp.int32, grid_shape, 2)
    span_ids = lax.broadcasted_iota(jnp.int32, grid_shape, 0)
    in_band = (col_ids > row_ids) & (col_ids <= row_ids + WINDOW)
    score_scale = 1.0 / math.sqrt(head_dim)
    pieces = []
    for block_index in range(span_rows // WINDOW):
        start = block_index * WINDOW
        query_rows = query_local[:, start : start + WINDOW]
        key_block = wide_keys[:, start : start + 2 * WINDOW]
        value_block = wide_values[:, start : start + 2 * WINDOW]
        scores = (
            jnp.einsum("cnd,cmd->cnm", query_rows, key_block, preferred_element_type=jnp.float32)
            * score_scale
        )
        allowed = in_band & ((col_ids + start >= WINDOW) | (span_ids > 0) | (seq_index > 0))
        scores = jnp.where(allowed, scores, -1e30)
        row_max = jnp.max(scores, axis=2, keepdims=True)
        exponent = jnp.exp(scores - row_max)
        probability = (exponent / jnp.sum(exponent, axis=2, keepdims=True)).astype(jnp.bfloat16)
        pieces.append(
            jnp.einsum("cnm,cmd->cnd", probability, value_block, preferred_element_type=jnp.float32)
        )
    return jnp.concatenate(pieces, axis=1)


def body(queries, key_rows, values, learn_rates, fast_gate, fast_down, fast_up, output_weight):
    query_local = queries[:, :, 0, :]
    key_local = key_rows[:, :, 0, :]
    value_local = values[:, :, 0, :]
    rate_local = learn_rates[0]
    span_rows = query_local.shape[1]
    seq_index = lax.axis_index(SEQ)
    clip_bound = 0.6 * math.sqrt(fast_gate.shape[2])
    edge_pair = passed_along(
        (key_local[:, span_rows - WINDOW :], value_local[:, span_rows - WINDOW :]), SEQ, 1
    )
    window_out = window_attend(query_local, key_local, value_local, edge_pair, seq_index)
    weights = (fast_gate[0], fast_down[0], fast_up[0])
    current = tuple((matrix.astype(jnp.bfloat16) for matrix in weights))
    momentum = None
    results = []
    for span_index in range(query_local.shape[0]):
        gradient = span_gradient(
            key_local[span_index], value_local[span_index], rate_local[span_index], current
        )
        summed = lax.psum((gradient[0], gradient[1], gradient[2]), SEQ)
        factor = jnp.minimum(1.0, clip_bound / jnp.sqrt(square_sum(summed) + 1e-06))
        momentum = advance(momentum, summed, factor)
        weights = tuple((matrix - change for matrix, change in zip(weights, momentum)))
        current = tuple((matrix.astype(jnp.bfloat16) for matrix in weights))
        results.append(apply_fast(query_local[span_index], current))
    fast_out = jnp.stack(results)
    combined = (fast_out + window_out).astype(jnp.bfloat16)
    head_block = whole_of(output_weight, SEQ, (0, 1), 1)
    return jnp.einsum(
        "cnf,fg->cng",
        lax.all_gather(combined, "head", axis=2, tiled=True),
        head_block,
        preferred_element_type=jnp.float32,
    ).astype(jnp.bfloat16)


def solution(mesh):
    torus = Mesh(mesh.devices.reshape(mesh.shape["head"], 4, 16), ("head", "seq_0", "seq_1"))
    placed = (
        P(None, SEQ, "head", None),
        P(None, SEQ, "head", None),
        P(None, SEQ, "head", None),
        P("head", None, SEQ),
        P("head", None, None),
        P("head", None, None),
        P("head", None, None),
        P(None, HEAD_SEQ),
    )
    return jax.shard_map(
        body, mesh=torus, in_specs=placed, out_specs=P(None, SEQ, "head"), check_vma=False
    )
```

profile of v0, /device:TPU:1, one launch (start us, length us, event | category | flops | bytes accessed | tf_op | source)
XLA Modules:
  0.0 653.0 jit_solution(61189129542604908)
XLA Ops:
  11.0 1.5 fusion.50
  13.9 1.4 convolution_bitcast_fusion.9
  17.1 274.4 %all-reduce.7.cloned.1.call-done = (f32[256,512]{0,1:T(8,128)}, f32[512,256]{1,0:T(8,128)}, f32[256,512]{0,1:T(8,128)}) async-done(((f32[256,512]{0,1:T(8,128)}, f32[512,256]{1,0:T(8,128)}, f32[256,512]{0,1:T(8,128)}), (f32[256,512]{0,1:T(8,128)}, f32[512,256]{1,0:T(8,128)}, f32[256,512]{0,1:T(8,128)})) %all-reduce.7.cloned.1.call-update) | async-done | bytes 1572880 | tf_op jit(solution)/shard_map/psum | solution.py:149
  291.5 1.8 multiply_reduce_fusion.6
  293.3 2.0 multiply_reduce_fusion.5
  305.5 3.3 collective-permute-start
  309.5 2.2 collective-permute-start.1
  311.8 9.9 %all-gather = bf16[8192,4]{0,1:T(4,128)(2,1)} all-gather(bf16[2048,4]{0,1:T(4,128)(2,1)S(1)} %copy-done.10), channel_id=2, replica_groups=mesh['head'=8,'seq_0'=4,'seq_1'=16] {'seq_0'}, dimensions={0}, use_global_device_ids=true | all-gather | bytes 81920 | tf_op jit(solution)/shard_map/all_gather | solution.py:32
  322.0 1.5 fusion.151
  323.6 2.3 fusion.6
  325.9 2.9 fusion.44
  331.7 2.6 fusion.156
  334.2 2.5 fusion.37
  338.1 2.8 multiply_reduce_fusion.4
  342.1 237.9 %all-reduce.5.cloned.1.call-done = (f32[256,512]{0,1:T(8,128)}, f32[512,256]{1,0:T(8,128)}, f32[256,512]{0,1:T(8,128)}) async-done(((f32[256,512]{0,1:T(8,128)}, f32[512,256]{1,0:T(8,128)}, f32[256,512]{0,1:T(8,128)}), (f32[256,512]{0,1:T(8,128)}, f32[512,256]{1,0:T(8,128)}, f32[256,512]{0,1:T(8,128)})) %all-reduce.5.cloned.1.call-update) | async-done | bytes 1572880 | tf_op jit(solution)/shard_map/psum | solution.py:149
  579.9 1.8 multiply_reduce_fusion.3
  581.7 1.8 multiply_reduce_fusion.2
  584.7 1.8 multiply_reduce_fusion.1
  587.2 2.5 convolution_bitcast_fusion.1
  589.6 3.3 multiply_reduce_fusion
  594.1 2.0 fusion.15
  596.1 1.8 copy.41
  598.1 43.1 %all-gather.5.cloned.1.call-done = bf16[2,512,2048]{1,2,0:T(8,128)(2,1)} async-done(((bf16[2,512,256]{1,2,0:T(8,128)(2,1)}), bf16[2,512,2048]{1,2,0:T(8,128)(2,1)}) %all-gather.5.cloned.1.call-update) | async-done | bytes 4194320 | tf_op jit(solution)/shard_map/all_gather | solution.py:160
  641.3 4.3 convolution_convert_fusion
  (64 shorter events, 22.7 us)
Async XLA Ops:
  7.4 5.2 copy-start.7
  7.4 284.1 %all-reduce.7.cloned.1.call-start = ((), (), s32[]{:S(2)}) async-start(), calls=%async_computation.3 | async-start | bytes 3145728 | tf_op jit(solution)/shard_map/psum | solution.py:149
  11.0 2.9 copy-start.1
  15.3 1.4 copy-start.3
  15.3 1.6 copy-start.4
  15.3 282.0 %copy-start.6 = (f32[1,512,256]{2,1,0:T(8,128)S(1)}, f32[1,512,256]{2,1,0:T(8,128)}, u32[]{:S(2)}) copy-start(f32[1,512,256]{2,1,0:T(8,128)} %param.13) | copy-start | bytes 1572868
  16.6 563.3 %all-reduce.5.cloned.1.call-start = ((), (), s32[]{:S(2)}) async-start(), calls=%async_computation.2 | async-start | bytes 3145728 | tf_op jit(solution)/shard_map/psum | solution.py:149
  291.5 8.4 %copy-start.2 = (f32[256,512]{0,1:T(8,128)S(1)}, f32[256,512]{0,1:T(8,128)}, u32[]{:S(2)}) copy-start(f32[256,512]{0,1:T(8,128)} %get-tuple-element.10) | copy-start | bytes 1572868
  303.5 8.3 %copy-start.10 = (bf16[2048,4]{0,1:T(4,128)(2,1)S(1)}, bf16[2048,4]{0,1:T(4,128)(2,1)}, u32[]{:S(2)}) copy-start(bf16[2048,4]{0,1:T(4,128)(2,1)} %param.15) | copy-start | bytes 49156
  304.8 291.3 %all-gather.7.cloned.1.call-start = ((), (), s32[]{:S(2)}) async-start(), calls=%async_computation.1 | async-start | bytes 1114112 | tf_op jit(solution)/shard_map/all_gather | solution.py:32
  305.5 23.2 %collective-permute-start = (bf16[2,256,256]{2,1,0:T(8,128)(2,1)}, bf16[2,256,256]{2,1,0:T(8,128)(2,1)}, u32[]{:S(2)}, u32[]{:S(2)}) collective-permute-start(bf16[2,256,256]{2,1,0:T(8,128)(2,1)} %slice.82), channel_id=1, source_target_pairs={{0,1},{1,2},{2,3},{3,4},{4,5},{5,6},{6,7},{7,8},{8,9},{9,10},{10,1... | collective-permute-start | bytes 786440 | tf_op jit(solution)/shard_map/ppermute | solution.py:20
  309.5 20.2 %collective-permute-start.1 = (bf16[2,256,256]{2,1,0:T(8,128)(2,1)}, bf16[2,256,256]{2,1,0:T(8,128)(2,1)}, u32[]{:S(2)}, u32[]{:S(2)}) collective-permute-start(bf16[2,256,256]{2,1,0:T(8,128)(2,1)} %slice.86), channel_id=1, source_target_pairs={{0,1},{1,2},{2,3},{3,4},{4,5},{5,6},{6,7},{7,8},{8,9},{9,10},{10,1... | collective-permute-start | bytes 786440 | tf_op jit(solution)/shard_map/ppermute | solution.py:20
  321.7 319.5 %all-gather.5.cloned.1.call-start = ((), (), s32[]{:S(2)}) async-start(), calls=%async_computation | async-start | bytes 4718592 | tf_op jit(solution)/shard_map/all_gather | solution.py:160
  334.2 2.5 copy-start.9
  338.0 249.1 %copy-start = (f32[256,512]{0,1:T(8,128)S(1)}, f32[256,512]{0,1:T(8,128)}, u32[]{:S(2)}) copy-start(f32[256,512]{0,1:T(8,128)} %get-tuple-element.8) | copy-start | bytes 1572868
  340.9 248.8 %copy-start.5 = (f32[512,256]{1,0:T(8,128)S(1)}, f32[512,256]{1,0:T(8,128)}, u32[]{:S(2)}) copy-start(f32[512,256]{1,0:T(8,128)} %get-tuple-element.9) | copy-start | bytes 1572868
  589.6 4.4 copy-start.8
Sparse Core Ops, SparseCore 0:
  16.7 274.6 all-reduce.6
  304.9 274.9 all-reduce.4
Sparse Core Ops, SparseCore 1:
  321.8 70.3 all-gather.6
  596.1 45.1 all-gather.4
where the time goes:
time: 654 us; the launch traced here: 653 us
  waiting for transfers between devices  555 us (85%)
  matrix products  39.5 us (6%)
  between operations  19 us (3%)
  other arithmetic  16.7 us (3%)
  blocking collectives  9.93 us (2%)
  local copies, waits for them, and re-layouts  6.7 us (1%)
    psum x2, waiting for transfers between devices, body(): summed = lax.psum((gradient[0], gradient[1], gradient[2]), SEQ)  512 us
    all_gather x1, waiting for transfers between devices, body(): lax.all_gather(combined, 'head', axis=2, tiled=True)  43.1 us
  transfers between devices with their start and end apart: 6, of which 3 were waited for; matrix products, arithmetic and copies ran while one was open for 6% of the time, Pallas kernels for 0%

commit v1 on v0

v1 whole, which is shorter than its diff:
```python
import math

import jax
import jax.numpy as jnp
from jax import lax
from jax.experimental import pallas as pl
from jax.experimental.pallas import tpu as pltpu
from jax.sharding import Mesh
from jax.sharding import PartitionSpec as P

WINDOW = 256
MOMENTUM = 0.9
TILE = 256
HEAD = ("y", "core")
SEQ = ("x", "z_hi", "z_lo")
SCOPED = pltpu.CompilerParams(vmem_limit_bytes=48 * 1024 * 1024)


def mm(left, right, dims):
    return lax.dot_general(left, right, (dims, ((), ())), preferred_element_type=jnp.float32)


def blocks_of(gate, down, up):
    halves = [slice(j * TILE, (j + 1) * TILE) for j in range(gate.shape[1] // TILE)]
    return [gate[:, h] for h in halves] + [down[h, :] for h in halves] + [up[:, h] for h in halves]


def clip_factor(total, clip_bound):
    return jnp.minimum(1.0, clip_bound / jnp.sqrt(total + 1e-06))


def factor_of(grad_ref, clip_bound):
    total = jnp.zeros((1, 1), jnp.float32)
    for t in range(grad_ref.shape[0] // TILE):
        piece = grad_ref[t * TILE : (t + 1) * TILE, :].astype(jnp.float32)
        total = total + jnp.sum(piece * piece, keepdims=True)
    return clip_factor(total, clip_bound)


def write_gradient(keys, values, rates, tiles, out_ref):
    count = len(tiles) // 3
    rate_column = jnp.transpose(jnp.broadcast_to(rates, (8, rates.shape[1])))[:, :1]
    target = (-(rate_column * values.astype(jnp.float32))).astype(jnp.bfloat16)
    for j in range(count):
        gate, down, up = tiles[j], tiles[count + j], tiles[2 * count + j]
        pre_gate = mm(keys, gate, ((1,), (0,)))
        pre_up = mm(keys, up, ((1,), (0,)))
        back = mm(target, down, ((1,), (1,)))
        sigmoid = jax.nn.sigmoid(pre_gate)
        silu = pre_gate * sigmoid
        hidden = (silu * pre_up).astype(jnp.bfloat16)
        slope = sigmoid * (1.0 + pre_gate * (1.0 - sigmoid))
        grad_pre_gate = (back * pre_up * slope).astype(jnp.bfloat16)
        grad_pre_up = (back * silu).astype(jnp.bfloat16)
        for place, left, right in (
            (j, keys, grad_pre_gate),
            (count + j, hidden, target),
            (2 * count + j, keys, grad_pre_up),
        ):
            out_ref[place * TILE : (place + 1) * TILE, :] = mm(left, right, ((0,), (0,))).astype(
                out_ref.dtype
            )


def fast_norm(queries, tiles):
    count = len(tiles) // 3
    fast = None
    for j in range(count):
        pre_gate = mm(queries, tiles[j], ((1,), (0,)))
        pre_up = mm(queries, tiles[2 * count + j], ((1,), (0,)))
        hidden = (pre_gate * jax.nn.sigmoid(pre_gate) * pre_up).astype(jnp.bfloat16)
        part = mm(hidden, tiles[count + j], ((1,), (0,)))
        fast = part if fast is None else fast + part
    return fast * lax.rsqrt(jnp.mean(fast * fast, axis=-1, keepdims=True) + 1e-05)


def first_gradient_kernel(keys_ref, values_ref, rates_ref, gate_ref, down_ref, up_ref, out_ref):
    tiles = [t.astype(jnp.bfloat16) for t in blocks_of(gate_ref, down_ref, up_ref)]
    write_gradient(keys_ref[0], values_ref[0], rates_ref[0:1], tiles, out_ref)


def second_gradient_kernel(
    clip_bound, keys_ref, values_ref, rates_ref, gate_ref, down_ref, up_ref, grad_ref, out_ref, low_ref
):
    factor = factor_of(grad_ref, clip_bound)
    tiles = []
    for t, start in enumerate(blocks_of(gate_ref, down_ref, up_ref)):
        rows = slice(t * TILE, (t + 1) * TILE)
        low = (start - factor * grad_ref[rows, :].astype(jnp.float32)).astype(jnp.bfloat16)
        low_ref[rows, :] = low
        tiles.append(low)
    write_gradient(keys_ref[1], values_ref[1], rates_ref[1:2], tiles, out_ref)


def first_apply_kernel(queries_ref, low_ref, window_ref, out_ref):
    tiles = [low_ref[t * TILE : (t + 1) * TILE, :] for t in range(low_ref.shape[0] // TILE)]
    out_ref[...] = (fast_norm(queries_ref[0], tiles) + window_ref[0]).astype(out_ref.dtype)


def second_apply_kernel(
    clip_bound, queries_ref, gate_ref, down_ref, up_ref, first_ref, second_ref, window_ref, out_ref
):
    factor_first = factor_of(first_ref, clip_bound)
    factor_second = factor_of(second_ref, clip_bound)
    tiles = []
    for t, start in enumerate(blocks_of(gate_ref, down_ref, up_ref)):
        rows = slice(t * TILE, (t + 1) * TILE)
        momentum = factor_first * first_ref[rows, :].astype(jnp.float32)
        weights = start - momentum
        momentum = MOMENTUM * momentum + factor_second * second_ref[rows, :].astype(jnp.float32)
        tiles.append((weights - momentum).astype(jnp.bfloat16))
    out_ref[...] = (fast_norm(queries_ref[1], tiles) + window_ref[1]).astype(out_ref.dtype)


def window_kernel(first_ref, queries_ref, keys_ref, values_ref, edges_ref, out_ref):
    is_first = first_ref[0]
    spans, span_rows, head_dim = queries_ref.shape
    scale = 1.0 / math.sqrt(head_dim)
    shape = (WINDOW, 2 * WINDOW)
    row_ids = lax.broadcasted_iota(jnp.int32, shape, 0)
    col_ids = lax.broadcasted_iota(jnp.int32, shape, 1)
    in_band = (col_ids > row_ids) & (col_ids <= row_ids + WINDOW)
    for c in range(spans):
        edge_keys, edge_values = edges_ref[0, c], edges_ref[1, c]
        if c > 0:
            edge_keys = jnp.where(is_first == 1, edges_ref[0, c - 1], edge_keys)
            edge_values = jnp.where(is_first == 1, edges_ref[1, c - 1], edge_values)
        for start in range(0, span_rows, WINDOW):
            here = slice(start, start + WINDOW)
            before = slice(start - WINDOW, start)
            past_keys = keys_ref[c, before] if start else edge_keys
            past_values = values_ref[c, before] if start else edge_values
            query_rows = queries_ref[c, here]
            allowed = in_band
            if c == 0 and start == 0:
                allowed = in_band & (col_ids >= WINDOW * is_first)
            scores = jnp.concatenate(
                [
                    mm(query_rows, past_keys, ((1,), (1,))),
                    mm(query_rows, keys_ref[c, here], ((1,), (1,))),
                ],
                axis=1,
            )
            scores = jnp.where(allowed, scores * scale, -1e30)
            exponent = jnp.exp(scores - jnp.max(scores, axis=1, keepdims=True))
            probability = exponent / jnp.sum(exponent, axis=1, keepdims=True)
            probability = probability.astype(jnp.bfloat16)
            out_ref[c, here] = mm(probability[:, :WINDOW], past_values, ((1,), (0,))) + mm(
                probability[:, WINDOW:], values_ref[c, here], ((1,), (0,))
            )


def first_project_kernel(mixed_ref, weight_ref, out_ref):
    out_ref[...] = project(mixed_ref, weight_ref).astype(out_ref.dtype)


def project(mixed_ref, weight_ref):
    total = None
    for h in range(mixed_ref.shape[0]):
        width = mixed_ref.shape[2]
        part = mm(mixed_ref[h], weight_ref[:, h * width : (h + 1) * width], ((1,), (1,)))
        total = part if total is None else total + part
    return total


def whole(kernel, out_shape, *operands, name):
    return pl.pallas_call(kernel, out_shape=out_shape, compiler_params=SCOPED, name=name)(*operands)


def reduced(gradient):
    rows, width = gradient.shape
    pieces = lax.all_to_all(gradient.reshape(4, rows // 4, width), "x", 0, 0)
    part = jnp.sum(pieces.astype(jnp.float32), axis=0).astype(jnp.bfloat16)
    pieces = lax.all_to_all(part.reshape(4, rows // 16, width), "z_lo", 0, 0)
    part = jnp.sum(pieces.astype(jnp.float32), axis=0).astype(jnp.bfloat16)
    pieces = lax.all_gather(part, "z_hi")
    part = jnp.sum(pieces.astype(jnp.float32), axis=0).astype(jnp.bfloat16)
    part = lax.all_gather(part, "z_lo", tiled=True)
    return lax.all_gather(part, "x", tiled=True)


def body(queries, key_rows, values, learn_rates, fast_gate, fast_down, fast_up, output_weight):
    queries = queries[:, :, 0, :]
    keys = key_rows[:, :, 0, :]
    values = values[:, :, 0, :]
    rates = learn_rates[0]
    weights = (fast_gate[0], fast_down[0], fast_up[0])
    spans, span_rows, width = queries.shape
    hid = weights[0].shape[1]
    clip_bound = 0.6 * math.sqrt(hid)
    flat = jax.ShapeDtypeStruct((3 * hid, width), jnp.bfloat16)
    mixed_shape = jax.ShapeDtypeStruct((span_rows, width), jnp.bfloat16)

    local = whole(first_gradient_kernel, flat, keys, values, rates, *weights, name="grad_0")

    seq_count = lax.axis_size(SEQ)
    edges = lax.ppermute(
        jnp.stack([keys[:, span_rows - WINDOW :], values[:, span_rows - WINDOW :]]),
        SEQ,
        [(i, (i + 1) % seq_count) for i in range(seq_count)],
    )
    is_first = (lax.axis_index(SEQ) == 0).astype(jnp.int32).reshape(1)
    window = pl.pallas_call(
        window_kernel,
        out_shape=jax.ShapeDtypeStruct(queries.shape, jnp.float32),
        in_specs=[pl.BlockSpec(memory_space=pltpu.SMEM)]
        + [pl.BlockSpec(memory_space=pltpu.VMEM)] * 4,
        compiler_params=SCOPED,
        name="window",
    )(is_first, queries, keys, values, edges)
    weight_rows = lax.all_gather(output_weight.T, SEQ, axis=0, tiled=True)

    first = reduced(local)
    local, low = whole(
        lambda *refs: second_gradient_kernel(clip_bound, *refs),
        (flat, flat),
        keys,
        values,
        rates,
        *weights,
        first,
        name="grad_1",
    )
    mixed = whole(first_apply_kernel, mixed_shape, queries, low, window, name="apply_0")
    gathered_first = lax.all_gather(mixed, HEAD)
    second = reduced(local)
    mixed = whole(
        lambda *refs: second_apply_kernel(clip_bound, *refs),
        mixed_shape,
        queries,
        *weights,
        first,
        second,
        window,
        name="apply_1",
    )
    gathered_second = lax.all_gather(mixed, HEAD)

    def project_kernel(first_ref, second_ref, weight_ref, out_ref):
        out_ref[0] = project(first_ref, weight_ref).astype(out_ref.dtype)
        out_ref[1] = project(second_ref, weight_ref).astype(out_ref.dtype)

    return whole(
        project_kernel,
        jax.ShapeDtypeStruct((spans, span_rows, width), jnp.bfloat16),
        gathered_first,
        gathered_second,
        weight_rows,
        name="project",
    )


def solution(mesh):
    z = math.isqrt(mesh.shape["seq"] // 4)
    torus = Mesh(mesh.devices.reshape(mesh.shape["head"] // 2, 2, 4, z, z), HEAD + SEQ)
    placed = (
        P(None, SEQ, HEAD, None),
        P(None, SEQ, HEAD, None),
        P(None, SEQ, HEAD, None),
        P(HEAD, None, SEQ),
        P(HEAD, None, None),
        P(HEAD, None, None),
        P(HEAD, None, None),
        P(None, HEAD + SEQ),
    )
    return jax.shard_map(
        body, mesh=torus, in_specs=placed, out_specs=P(None, SEQ, HEAD), check_vma=False
    )
```

time: 654 us -> 238 us (0.36)
  waiting for transfers between devices: 555 us -> 75.3 us
  blocking collectives: 9.93 us -> 99.7 us
  matrix products: 39.5 us -> 0 us
  other arithmetic: 16.7 us -> 4.85 us
  starting transfers between devices: 5.79 us -> 16.9 us
  Pallas kernels: 0 us -> 10.7 us
  local copies, waits for them, and re-layouts: 6.7 us -> 16.3 us
    psum x2 -> x0, waiting for transfers between devices: 512 us -> none  [body(): summed = lax.psum((gradient[0], gradient[1], gradient[2]), SEQ)]
    all_gather x1 -> x6, blocking collectives: 9.93 us -> 77 us  [the longest x2 31.9 us: reduced(): pieces = lax.all_gather(part, 'z_hi')]
    dot_general x20 -> x0, matrix products: 35.4 us -> none  [the longest x6 8.12 us: contract_rows(): lax.dot_general(left, right, (((0,), (0,)), ((), ())), preferred_element_...]
    all_to_all x0 -> x2, blocking collectives: none -> 22.7 us  [the longest x1 12.9 us: reduced(): pieces = lax.all_to_all(gradient.reshape(4, rows // 4, width), 'x', 0, 0)]
    ppermute x2 -> x1, waiting for transfers between devices: 0.01 us -> 18.1 us  [body(): lax.ppermute(jnp.stack([keys[:, span_rows - WINDOW:], values[:, span_rows...]
    unnamed x24 -> x41, local copies, waits for them, and re-layouts: 0.44 us -> 16.3 us
    all_to_all x0 -> x2, starting transfers between devices: none -> 13.5 us  [the longest x1 8.7 us: reduced(): pieces = lax.all_to_all(part.reshape(4, rows // 16, width), 'z_lo', 0, 0)]
    pallas_call x0 -> x6, Pallas kernels: none -> 10.7 us  [the longest x5 9.33 us: whole(): pl.pallas_call(kernel, out_shape=out_shape, compiler_params=SCOPED, name=...]
  transfers between devices with their start and end apart: 6 -> 6, of which waited for: 3 -> 4; matrix products, arithmetic and copies ran while one was open for 6% -> 3% of each run, Pallas kernels for 0% -> 4%
where the time goes in v1:
time: 238 us; the launch traced here: 237 us
  blocking collectives  99.7 us (42%)
  waiting for transfers between devices  75.3 us (32%)
  starting transfers between devices  16.9 us (7%)
  local copies, waits for them, and re-layouts  16.3 us (7%)
  between operations  13.3 us (6%)
  Pallas kernels  10.7 us (4%)
  other arithmetic  4.85 us (2%)
    all_gather x1, waiting for transfers between devices, body(): gathered_second = lax.all_gather(mixed, HEAD)  38.1 us
    all_gather x2, blocking collectives, reduced(): pieces = lax.all_gather(part, 'z_hi')  31.9 us
    all_gather x2, blocking collectives, reduced(): part = lax.all_gather(part, 'z_lo', tiled=True)  24 us
    all_gather x2, blocking collectives, reduced(): return lax.all_gather(part, 'x', tiled=True)  21.1 us
    ppermute x1, waiting for transfers between devices, body(): lax.ppermute(jnp.stack([keys[:, span_rows - WINDOW:], values[:, span_rows...  18.1 us
    unnamed x41, local copies, waits for them, and re-layouts  16.3 us
    all_to_all x1, blocking collectives, reduced(): pieces = lax.all_to_all(gradient.reshape(4, rows // 4, width), 'x', 0, 0)  12.9 us
    all_gather x1, waiting for transfers between devices, body(): gathered_first = lax.all_gather(mixed, HEAD)  10.1 us
  transfers between devices with their start and end apart: 6, of which 4 were waited for; matrix products, arithmetic and copies ran while one was open for 3% of the time, Pallas kernels for 4%

profile of v1, /device:TPU:1, one launch (start us, length us, event | category | flops | bytes accessed | tf_op | source)
XLA Modules:
  0.0 237.1 jit_solution(8274357431883460047)
XLA Ops:
  13.2 2.4 %grad_0.1 = bf16[1536,256]{1,0:T(8,128)(2,1)} custom-call(bf16[2,512,256]{2,1,0:T(8,128)(2,1)S(1)} %bitcast.23, bf16[2,512,256]{2,1,0:T(8,128)(2,1)S(1)} %bitcast.27, f32[2,512]{1,0:T(2,128)S(1)} %bitcast.46, f32[256,512]{1,0:T(8,128)S(1)} %bitcast.34, f32[512,256]{1,0:T(8,128)S(1)} %bitcast.37, f32[256,512]{1,0:T(8,128)S(1)} %bitcast.40), custom_call_target="tpu_custom_call" | custom-call | tf_op jit(solution)/shard_map/grad_0/pallas_call | solution.py:167
  15.5 4.8 %all-to-all-start = ((bf16[4,384,256]{2,1,0:T(8,128)(2,1)}), bf16[4,384,256]{2,1,0:T(8,128)(2,1)S(1)}, u32[]{:S(2)}, u32[]{:S(2)}) async-start(bf16[4,384,256]{2,1,0:T(8,128)(2,1)} %bitcast.7), calls=%async_computation | async-start | bytes 1572864 | tf_op jit(solution)/shard_map/all_to_all | solution.py:172
  20.4 8.3 %all-to-all-done = bf16[4,384,256]{2,1,0:T(8,128)(2,1)S(1)} async-done(((bf16[4,384,256]{2,1,0:T(8,128)(2,1)}), bf16[4,384,256]{2,1,0:T(8,128)(2,1)S(1)}, u32[]{:S(2)}, u32[]{:S(2)}) %all-to-all-start) | async-done | bytes 786464 | tf_op jit(solution)/shard_map/all_to_all | solution.py:172
  29.5 8.7 %all-to-all-start.1 = ((bf16[4,96,256]{2,1,0:T(8,128)(2,1)}), bf16[4,96,256]{2,1,0:T(8,128)(2,1)S(1)}, u32[]{:S(2)}, u32[]{:S(2)}) async-start(bf16[4,96,256]{2,1,0:T(8,128)(2,1)} %bitcast.8), calls=%async_computation.1 | async-start | bytes 393216 | tf_op jit(solution)/shard_map/all_to_all | solution.py:174
  38.3 3.4 %collective-permute-start = (bf16[2,2,256,256]{3,2,1,0:T(8,128)(2,1)S(1)}, bf16[2,2,256,256]{3,2,1,0:T(8,128)(2,1)S(1)}, u32[]{:S(2)}, u32[]{:S(2)}) collective-permute-start(bf16[2,2,256,256]{3,2,1,0:T(8,128)(2,1)S(1)} %pad_maximum_fusion), channel_id=1, source_target_pairs={{0,1},{1,2},{2,3},{3,4},{4,5},{5,6},{6,7},{7,8},{8,9},{9,10},{10,1... | collective-permute-start | bytes 1572872 | tf_op jit(solution)/shard_map/ppermute | solution.py:197
  41.7 18.1 %collective-permute-done.edges_ref = bf16[2,2,256,256]{3,2,1,0:T(8,128)(2,1)S(1)} collective-permute-done((bf16[2,2,256,256]{3,2,1,0:T(8,128)(2,1)S(1)}, bf16[2,2,256,256]{3,2,1,0:T(8,128)(2,1)S(1)}, u32[]{:S(2)}, u32[]{:S(2)}) %collective-permute-start) | collective-permute-done | bytes 524320 | tf_op jit(solution)/shard_map/ppermute | solution.py:197
  59.8 1.4 window.1.window_ref.refs_6_
  61.2 15.8 %all-gather = bf16[384,256]{1,0:T(8,128)(2,1)S(1)} all-gather(bf16[96,256]{1,0:T(8,128)(2,1)S(1)} %reduce_sum.73), channel_id=2, replica_groups=mesh['y'=4,'core'=2,'x'=4,'z_hi'=4,'z_lo'=4] {'z_hi'}, dimensions={0}, use_global_device_ids=true | all-gather | bytes 245760 | tf_op jit(solution)/shard_map/all_gather | solution.py:176
  77.1 12.5 %all_gather.41 = bf16[384,256]{1,0:T(8,128)(2,1)S(1)} all-gather(bf16[96,256]{1,0:T(8,128)(2,1)S(1)} %reduce_sum.74), channel_id=1, replica_groups=mesh['y'=4,'core'=2,'x'=4,'z_hi'=4,'z_lo'=4] {'z_lo'}, dimensions={0}, use_global_device_ids=true | all-gather | bytes 245760 | tf_op jit(solution)/shard_map/all_gather | solution.py:178
  89.6 10.7 %all_gather.42.refs_6_.refs_4_ = bf16[1536,256]{1,0:T(8,128)(2,1)S(1)} all-gather(bf16[384,256]{1,0:T(8,128)(2,1)S(1)} %all_gather.41), channel_id=1, replica_groups=mesh['y'=4,'core'=2,'x'=4,'z_hi'=4,'z_lo'=4] {'x'}, dimensions={0}, use_global_device_ids=true | all-gather | bytes 983040 | tf_op jit(solution)/shard_map/all_gather | solution.py:179
  103.5 1.8 grad_1.1
  106.2 1.6 apply_0.1
  107.9 12.9 %all_to_all.20 = bf16[4,384,256]{2,1,0:T(8,128)(2,1)} all-to-all(bf16[4,384,256]{2,1,0:T(8,128)(2,1)} %bitcast.45), channel_id=1, replica_groups=mesh['y'=4,'core'=2,'x'=4,'z_hi'=4,'z_lo'=4] {'x'}, dimensions={0} | all-to-all | bytes 1572864 | tf_op jit(solution)/shard_map/all_to_all | solution.py:172
  120.8 2.0 reduce_sum.75
  122.8 9.8 %all_to_all.21 = bf16[4,96,256]{2,1,0:T(8,128)(2,1)} all-to-all(bf16[4,96,256]{2,1,0:T(8,128)(2,1)} %bitcast.48), channel_id=1, replica_groups=mesh['y'=4,'core'=2,'x'=4,'z_hi'=4,'z_lo'=4] {'z_lo'}, dimensions={0} | all-to-all | bytes 393216 | tf_op jit(solution)/shard_map/all_to_all | solution.py:174
  133.5 16.1 %all-gather.2 = bf16[384,256]{1,0:T(8,128)(2,1)} all-gather(bf16[96,256]{1,0:T(8,128)(2,1)S(1)} %reduce_sum.76), channel_id=4, replica_groups=mesh['y'=4,'core'=2,'x'=4,'z_hi'=4,'z_lo'=4] {'z_hi'}, dimensions={0}, use_global_device_ids=true | all-gather | bytes 245760 | tf_op jit(solution)/shard_map/all_gather | solution.py:176
  150.6 11.4 %all_gather.47 = bf16[384,256]{1,0:T(8,128)(2,1)S(1)} all-gather(bf16[96,256]{1,0:T(8,128)(2,1)S(1)} %reduce_sum.77), channel_id=1, replica_groups=mesh['y'=4,'core'=2,'x'=4,'z_hi'=4,'z_lo'=4] {'z_lo'}, dimensions={0}, use_global_device_ids=true | all-gather | bytes 245760 | tf_op jit(solution)/shard_map/all_gather | solution.py:178
  162.0 10.4 %all_gather.48.refs_5_ = bf16[1536,256]{1,0:T(8,128)(2,1)S(1)} all-gather(bf16[384,256]{1,0:T(8,128)(2,1)S(1)} %all_gather.47), channel_id=1, replica_groups=mesh['y'=4,'core'=2,'x'=4,'z_hi'=4,'z_lo'=4] {'x'}, dimensions={0}, use_global_device_ids=true | all-gather | bytes 983040 | tf_op jit(solution)/shard_map/all_gather | solution.py:179
  173.5 1.5 apply_1.1
  177.1 10.1 %all-gather.9.cloned.1.call-done = bf16[4096,256]{1,0:T(8,128)(2,1)} async-done(((bf16[512,256]{1,0:T(8,128)(2,1)}), bf16[4096,256]{1,0:T(8,128)(2,1)}) %all-gather.9.cloned.1.call-update) | async-done | bytes 2097168 | tf_op jit(solution)/shard_map/all_gather | solution.py:225
  187.2 38.1 %all-gather.11.cloned.1.call-done = bf16[4096,256]{1,0:T(8,128)(2,1)} async-done(((bf16[512,256]{1,0:T(8,128)(2,1)}), bf16[4096,256]{1,0:T(8,128)(2,1)}) %all-gather.11.cloned.1.call-update) | async-done | bytes 2097168 | tf_op jit(solution)/shard_map/all_gather | solution.py:237
  225.3 1.6 copy-done.14
  226.9 1.6 copy-done.15
  228.5 2.1 project.1
  (54 shorter events, 16.8 us)
Async XLA Ops:
  6.5 169.2 %all-gather.13.cloned.1.call-start = ((), (), s32[]{:S(2)}) async-start(), calls=%async_computation.6 | async-start | bytes 1064960 | tf_op jit(solution)/shard_map/all_gather | solution.py:211
  7.3 1.0 copy-start
  8.3 1.0 copy-start.2
  9.3 1.0 copy-start.5
  10.4 1.0 copy-start.8
  11.4 1.0 copy-start.11
  13.2 7.2 %copy-start.1 = (bf16[2,512,1,256]{3,1,2,0:T(8,128)(2,1)S(1)}, bf16[2,512,1,256]{3,1,2,0:T(8,128)(2,1)}, u32[]{:S(2)}) copy-start(bf16[2,512,1,256]{3,1,2,0:T(8,128)(2,1)} %param.9) | copy-start | bytes 1572868
  13.2 7.2 %copy-start.3 = (bf16[2,512,1,256]{3,1,2,0:T(8,128)(2,1)S(1)}, bf16[2,512,1,256]{3,1,2,0:T(8,128)(2,1)}, u32[]{:S(2)}) copy-start(bf16[2,512,1,256]{3,1,2,0:T(8,128)(2,1)} %param.10) | copy-start | bytes 1572868
  15.5 13.2 %all-to-all-start = ((bf16[4,384,256]{2,1,0:T(8,128)(2,1)}), bf16[4,384,256]{2,1,0:T(8,128)(2,1)S(1)}, u32[]{:S(2)}, u32[]{:S(2)}) async-start(bf16[4,384,256]{2,1,0:T(8,128)(2,1)} %bitcast.7), calls=%async_computation | async-start | bytes 1572864 | tf_op jit(solution)/shard_map/all_to_all | solution.py:172
  20.4 39.4 %copy-start.4 = (bf16[2,512,1,256]{3,1,2,0:T(8,128)(2,1)S(1)}, bf16[2,512,1,256]{3,1,2,0:T(8,128)(2,1)}, u32[]{:S(2)}) copy-start(bf16[2,512,1,256]{3,1,2,0:T(8,128)(2,1)} %param.8) | copy-start | bytes 1572868
  29.5 31.6 %all-to-all-start.1 = ((bf16[4,96,256]{2,1,0:T(8,128)(2,1)}), bf16[4,96,256]{2,1,0:T(8,128)(2,1)S(1)}, u32[]{:S(2)}, u32[]{:S(2)}) async-start(bf16[4,96,256]{2,1,0:T(8,128)(2,1)} %bitcast.8), calls=%async_computation.1 | async-start | bytes 393216 | tf_op jit(solution)/shard_map/all_to_all | solution.py:174
  38.2 149.0 %all-gather.9.cloned.1.call-start = ((), (), s32[]{:S(2)}) async-start(), calls=%async_computation.4 | async-start | bytes 2359296 | tf_op jit(solution)/shard_map/all_gather | solution.py:225
  38.3 21.5 %collective-permute-start = (bf16[2,2,256,256]{3,2,1,0:T(8,128)(2,1)S(1)}, bf16[2,2,256,256]{3,2,1,0:T(8,128)(2,1)S(1)}, u32[]{:S(2)}, u32[]{:S(2)}) collective-permute-start(bf16[2,2,256,256]{3,2,1,0:T(8,128)(2,1)S(1)} %pad_maximum_fusion), channel_id=1, source_target_pairs={{0,1},{1,2},{2,3},{3,4},{4,5},{5,6},{6,7},{7,8},{8,9},{9,10},{10,1... | collective-permute-start | bytes 1572872 | tf_op jit(solution)/shard_map/ppermute | solution.py:197
  59.8 40.5 %copy-start.19 = (f32[1,2,512]{2,1,0:T(2,128)S(1)}, f32[1,2,512]{2,1,0:T(2,128)}, u32[]{:S(2)}) copy-start(f32[1,2,512]{2,1,0:T(2,128)} %param.11) | copy-start | bytes 12292
  100.3 1.1 copy-start.6
  101.4 1.0 copy-start.9
  102.4 1.0 copy-start.12
  105.3 0.9 copy-start.17
  107.8 117.5 %all-gather.11.cloned.1.call-start = ((), (), s32[]{:S(2)}) async-start(), calls=%async_computation.5 | async-start | bytes 2359296 | tf_op jit(solution)/shard_map/all_gather | solution.py:237
  107.8 64.6 %copy-start.7 = (f32[1,256,512]{2,1,0:T(8,128)S(1)}, f32[1,256,512]{2,1,0:T(8,128)}, u32[]{:S(2)}) copy-start(f32[1,256,512]{2,1,0:T(8,128)} %param.12) | copy-start | bytes 1572868
  107.8 64.6 %copy-start.10 = (f32[1,512,256]{2,1,0:T(8,128)S(1)}, f32[1,512,256]{2,1,0:T(8,128)}, u32[]{:S(2)}) copy-start(f32[1,512,256]{2,1,0:T(8,128)} %param.13) | copy-start | bytes 1572868
  172.5 1.0 copy-start.13
  225.3 1.6 copy-start.14
  226.9 1.6 copy-start.15
  (2 other events, 1.4 us)
Sparse Core Ops, SparseCore 0:
  10.3 136.0 all-gather.12
  148.5 38.6 all-gather.8
  189.4 35.8 all-gather.10
